TPU v7x, 32 devices: a whole 2x2x4 slice. The times are simulated.
32 devices in a mesh: dp: 8 (over y, x, core), tensor: 4 (over z).
Axes of the slice: x: 2, y: 2, z: 4, core: 2. Of those that a mesh axis runs over, the one named last changes fastest.
Arguments:
- tokens: bfloat16 [8192, 2048], P(('dp', 'tensor')), may hold values from -6 to 6
- seq_start: int32 [8192], P('dp'), may hold values from 0 to 8191, as said below
- proj_weight: bfloat16 [2048, 3, 2048], P('dp', None, 'tensor'), may hold values from -0.125 to 0.125
- proj_bias: bfloat16 [3, 8, 256], P(None, 'tensor', 'dp'), may hold values from -3 to 3
- out_weight: bfloat16 [2048, 2048], P('tensor', 'dp'), may hold values from -1.5 to 1.5
- up_weight: bfloat16 [2048, 8192], P('dp', 'tensor'), may hold values from -0.125 to 0.125
- up_bias: bfloat16 [4, 2048], P('tensor', 'dp'), may hold values from -3 to 3
- down_weight: bfloat16 [8192, 2048], P('tensor', 'dp'), may hold values from -0.0625 to 0.0625
- norm_gains: bfloat16 [2, 2048], P(None, ('dp', 'tensor')), may hold values from 0.099609375 to 1.8984375
- biases: bfloat16 [4, 2048], P(None, ('dp', 'tensor')), may hold values from -3 to 3
- cotangent: bfloat16 [8192, 2048], P(('dp', 'tensor')), may hold values from -6 to 6
Outputs:
- output: bfloat16 [8192, 2048], P(('dp', 'tensor'))
- input_grad: float32 [8192, 2048], P(('dp', 'tensor'))
- proj_grad: float32 [2048, 3, 2048], P('dp', None, 'tensor')
- proj_bias_grad: float32 [3, 8, 256], P(None, 'tensor', 'dp')
- out_grad: float32 [2048, 2048], P('tensor', 'dp')
- up_grad: float32 [2048, 8192], P('dp', 'tensor')
- up_bias_grad: float32 [4, 2048], P('tensor', 'dp')
- down_grad: float32 [8192, 2048], P('tensor', 'dp')
- gains_grad: float32 [2, 2048], P(None, ('dp', 'tensor'))
- biases_grad: float32 [4, 2048], P(None, ('dp', 'tensor'))
Inputs may be any that keep to these rules, and one draw needn't show every extreme that they name: seq_start never falls along the tokens, is at most the token's own index, and every sequence lies inside one aligned block of 1024 tokens (the tokens of one index of dp); some block other than the last holds a single sequence of 1024 tokens, the others hold sequences of uneven lengths, and the last token begins a sequence of its own.
All inputs are finite; a program needn't handle non-finite values.
Results may differ from a plain program's by a relative error of at most 0.012.
Values may be sent and summed in bfloat16 or wider, within the bound.
No kernel may reach another device: no remote copies, remote signals or barrier semaphores. Data moves between devices by JAX's collectives and lax.ppermute only.
A program may use at most 192 MiB of HBM per device.

v0:
```python
import jax
import jax.numpy as jnp
from jax import lax
from jax.sharding import PartitionSpec as P

ROT = 64
EPSILON = 1e-05
ROTARY_BASE = 10000.0


def layer_norm(values, gain_row, shift_row):
    centered = values - jnp.mean(values, axis=-1, keepdims=True)
    spread = jnp.mean(centered * centered, axis=-1, keepdims=True)
    return centered * lax.rsqrt(spread + EPSILON) * gain_row + shift_row


def both_norms(values, gain_rows, shift_rows):
    return (
        layer_norm(values, gain_rows[0], shift_rows[0]),
        layer_norm(values, gain_rows[1], shift_rows[1]),
    )


def gelu_exact(inputs):
    return jax.nn.gelu(inputs, approximate=False)


def rotate(values, positions, turn_sign):
    half_rot = ROT // 2
    frequency = ROTARY_BASE ** (-(jnp.arange(half_rot, dtype=jnp.float32) * 2.0) / ROT)
    angles = positions.astype(jnp.float32)[:, None] * frequency[None, :]
    cosine = jnp.cos(angles)[:, None, :]
    sine_term = turn_sign * jnp.sin(angles)[:, None, :]
    first_half = values[..., :half_rot]
    second_half = values[..., half_rot:ROT]
    return jnp.concatenate(
        [
            first_half * cosine - second_half * sine_term,
            second_half * cosine + first_half * sine_term,
            values[..., ROT:],
        ],
        axis=-1,
    )


def masked_scores(query_block, key_rows, starts, block_start, block_rows):
    row_count = key_rows.shape[0]
    score_scale = key_rows.shape[-1] ** (-0.5)
    key_index = jnp.arange(row_count, dtype=jnp.int32)
    query_begin = lax.dynamic_slice_in_dim(starts, block_start, block_rows, 0)
    query_index = block_start + jnp.arange(block_rows, dtype=jnp.int32)
    scores = (
        jnp.einsum("qhe,khe->hqk", query_block, key_rows, preferred_element_type=jnp.float32)
        * score_scale
    )
    allowed = (query_begin[:, None] == starts[None, :]) & (
        key_index[None, :] <= query_index[:, None]
    )
    return jnp.where(allowed[None], scores, -1e30)


def attention_forward(queries, key_rows, value_rows, starts, block_rows):
    row_count = queries.shape[0]

    def one_block(block_start):
        query_block = lax.dynamic_slice_in_dim(queries, block_start, block_rows, 0)
        scores = masked_scores(query_block, key_rows, starts, block_start, block_rows)
        row_max = jnp.max(scores, axis=-1, keepdims=True)
        powers = jnp.exp(scores - row_max)
        row_total = jnp.sum(powers, axis=-1, keepdims=True)
        weights = (powers / row_total).astype(jnp.bfloat16)
        attended = jnp.einsum(
            "hqk,khe->qhe", weights, value_rows, preferred_element_type=jnp.float32
        )
        return (attended, (row_max + jnp.log(row_total))[..., 0])

    block_starts = jnp.arange(row_count // block_rows, dtype=jnp.int32) * block_rows
    attended, log_total = lax.map(one_block, block_starts)
    return (attended.reshape(queries.shape), log_total)


def attention_backward(queries, key_rows, value_rows, starts, log_total, grad_attended, block_rows):
    row_count = queries.shape[0]
    score_scale = queries.shape[-1] ** (-0.5)

    def one_block(accumulated, pieces):
        block_start, block_total = pieces
        grad_keys, grad_values = accumulated
        query_block = lax.dynamic_slice_in_dim(queries, block_start, block_rows, 0)
        grad_block = lax.dynamic_slice_in_dim(grad_attended, block_start, block_rows, 0)
        scores = masked_scores(query_block, key_rows, starts, block_start, block_rows)
        probs = jnp.exp(scores - block_total[..., None])
        grad_values = grad_values + jnp.einsum(
            "hqk,qhe->khe",
            probs.astype(jnp.bfloat16),
            grad_block,
            preferred_element_type=jnp.float32,
        )
        grad_probs = jnp.einsum(
            "qhe,khe->hqk", grad_block, value_rows, preferred_element_type=jnp.float32
        )
        inner_sum = jnp.sum(probs * grad_probs, axis=-1, keepdims=True)
        grad_scores = (probs * (grad_probs - inner_sum)).astype(jnp.bfloat16)
        grad_query = (
            jnp.einsum("hqk,khe->qhe", grad_scores, key_rows, preferred_element_type=jnp.float32)
            * score_scale
        )
        grad_keys = (
            grad_keys
            + jnp.einsum(
                "hqk,qhe->khe", grad_scores, query_block, preferred_element_type=jnp.float32
            )
            * score_scale
        )
        return ((grad_keys, grad_values), grad_query)

    block_starts = jnp.arange(row_count // block_rows, dtype=jnp.int32) * block_rows
    zeros_like_keys = jnp.zeros(queries.shape, jnp.float32)
    (grad_keys, grad_values), grad_queries = lax.scan(
        one_block, (zeros_like_keys, zeros_like_keys), (block_starts, log_total)
    )
    return (grad_queries.reshape(queries.shape), grad_keys, grad_values)


def shards(
    tokens,
    seq_start,
    proj_weight,
    proj_bias,
    out_weight,
    up_weight,
    up_bias,
    down_weight,
    norm_gains,
    biases,
    cotangent,
):
    local_rows = tokens.shape[0]
    row_count = local_rows * lax.axis_size("tensor")
    block_rows = min(512, row_count)
    dp_index = lax.axis_index("dp")
    gathered = (
        lax.all_gather(proj_weight, "dp", axis=0, tiled=True),
        lax.all_gather(proj_bias, "dp", axis=2, tiled=True),
        lax.all_gather(out_weight, "dp", axis=1, tiled=True),
        lax.all_gather(up_weight, "dp", axis=0, tiled=True),
        lax.all_gather(up_bias, "dp", axis=1, tiled=True),
        lax.all_gather(down_weight, "dp", axis=1, tiled=True),
    )
    joined_weight, joined_bias, mix_weight, hidden_weight, hidden_bias, back_weight = gathered
    gain_rows, shift_rows = (
        lax.all_gather(norm_gains, ("dp", "tensor"), axis=1, tiled=True),
        lax.all_gather(biases, ("dp", "tensor"), axis=1, tiled=True),
    )
    gain_rows = gain_rows.astype(jnp.float32)
    shift_rows = shift_rows.astype(jnp.float32)
    local_f = tokens.astype(jnp.float32)
    first_local, second_local = both_norms(local_f, gain_rows, shift_rows)
    first_rows, second_rows = (
        lax.all_gather(first_local.astype(jnp.bfloat16), "tensor", axis=0, tiled=True),
        lax.all_gather(second_local.astype(jnp.bfloat16), "tensor", axis=0, tiled=True),
    )
    heads_here = joined_bias.shape[1]
    head_size = joined_bias.shape[2]
    local_width = heads_here * head_size
    projected = jnp.einsum(
        "nd,dch->nch", first_rows, joined_weight, preferred_element_type=jnp.float32
    ) + joined_bias.astype(jnp.float32).reshape(3, local_width)
    positions = dp_index * row_count + jnp.arange(row_count, dtype=jnp.int32) - seq_start
    queries = rotate(
        projected[:, 0].reshape(row_count, heads_here, head_size), positions, 1.0
    ).astype(jnp.bfloat16)
    key_rows = rotate(
        projected[:, 1].reshape(row_count, heads_here, head_size), positions, 1.0
    ).astype(jnp.bfloat16)
    value_rows = projected[:, 2].reshape(row_count, heads_here, head_size).astype(jnp.bfloat16)
    attended, log_total = attention_forward(queries, key_rows, value_rows, seq_start, block_rows)
    attended = attended.reshape(row_count, local_width).astype(jnp.bfloat16)
    hidden = jnp.dot(
        second_rows, hidden_weight, preferred_element_type=jnp.float32
    ) + hidden_bias.astype(jnp.float32)
    activated = gelu_exact(hidden).astype(jnp.bfloat16)
    attn_part = jnp.dot(attended, mix_weight, preferred_element_type=jnp.float32)
    branches = lax.psum_scatter(
        attn_part + jnp.dot(activated, back_weight, preferred_element_type=jnp.float32),
        "tensor",
        scatter_dimension=0,
        tiled=True,
    )
    output = (local_f + branches + shift_rows[2] + shift_rows[3]).astype(jnp.bfloat16)
    grad_rows = lax.all_gather(cotangent, "tensor", axis=0, tiled=True)
    regathered = (
        lax.all_gather(proj_weight, "dp", axis=0, tiled=True),
        lax.all_gather(proj_bias, "dp", axis=2, tiled=True),
        lax.all_gather(out_weight, "dp", axis=1, tiled=True),
        lax.all_gather(up_weight, "dp", axis=0, tiled=True),
        lax.all_gather(up_bias, "dp", axis=1, tiled=True),
        lax.all_gather(down_weight, "dp", axis=1, tiled=True),
    )
    joined_again, _, mix_again, hidden_again, _, back_again = regathered
    grad_active = jnp.einsum("nd,fd->nf", grad_rows, back_again, preferred_element_type=jnp.float32)
    down_term = jnp.einsum("nf,nd->fd", activated, grad_rows, preferred_element_type=jnp.float32)
    _, gelu_back = jax.vjp(gelu_exact, hidden)
    grad_hidden = gelu_back(grad_active)[0].astype(jnp.bfloat16)
    up_term = jnp.einsum("nd,nf->df", second_rows, grad_hidden, preferred_element_type=jnp.float32)
    up_bias_term = jnp.sum(grad_hidden, axis=0, keepdims=True, dtype=jnp.float32)
    grad_second = jnp.einsum(
        "nf,df->nd", grad_hidden, hidden_again, preferred_element_type=jnp.float32
    )
    grad_attended = jnp.einsum(
        "nd,ed->ne", grad_rows, mix_again, preferred_element_type=jnp.float32
    ).astype(jnp.bfloat16)
    mix_term = jnp.einsum("ne,nd->ed", attended, grad_rows, preferred_element_type=jnp.float32)
    query_back, key_back, value_back = attention_backward(
        queries,
        key_rows,
        value_rows,
        seq_start,
        log_total,
        grad_attended.reshape(row_count, heads_here, head_size),
        block_rows,
    )
    query_back = rotate(query_back, positions, -1.0).reshape(row_count, local_width)
    key_back = rotate(key_back, positions, -1.0).reshape(row_count, local_width)
    grad_projected = jnp.stack(
        [query_back, key_back, value_back.reshape(row_count, local_width)], axis=1
    ).astype(jnp.bfloat16)
    joined_term = jnp.einsum(
        "nd,nch->dch", first_rows, grad_projected, preferred_element_type=jnp.float32
    )
    joined_bias_term = jnp.sum(grad_projected, axis=0, dtype=jnp.float32).reshape(
        3, heads_here, head_size
    )
    grad_first = jnp.einsum(
        "nch,dch->nd", grad_projected, joined_again, preferred_element_type=jnp.float32
    )
    grad_local = cotangent.astype(jnp.float32)
    first_sum, second_sum = (
        lax.psum_scatter(
            grad_first.astype(jnp.bfloat16), "tensor", scatter_dimension=0, tiled=True
        ).astype(jnp.float32),
        lax.psum_scatter(
            grad_second.astype(jnp.bfloat16), "tensor", scatter_dimension=0, tiled=True
        ).astype(jnp.float32),
    )
    _, norm_back = jax.vjp(both_norms, local_f, gain_rows, shift_rows)
    grad_norm_in, gain_term, shift_term = norm_back((first_sum, second_sum))
    input_grad = grad_local + grad_norm_in
    column_sums = jnp.sum(grad_local, axis=0)
    shift_term = jnp.concatenate([shift_term[:2], jnp.stack([column_sums, column_sums])], axis=0)
    gains_grad, biases_grad = (
        lax.psum_scatter(gain_term, ("dp", "tensor"), scatter_dimension=1, tiled=True),
        lax.psum_scatter(shift_term, ("dp", "tensor"), scatter_dimension=1, tiled=True),
    )
    summed = (
        lax.psum_scatter(joined_term, "dp", scatter_dimension=0, tiled=True),
        lax.psum_scatter(joined_bias_term, "dp", scatter_dimension=2, tiled=True),
        lax.psum_scatter(mix_term, "dp", scatter_dimension=1, tiled=True),
        lax.psum_scatter(up_term, "dp", scatter_dimension=0, tiled=True),
        lax.psum_scatter(up_bias_term, "dp", scatter_dimension=1, tiled=True),
        lax.psum_scatter(down_term, "dp", scatter_dimension=1, tiled=True),
    )
    return (
        output,
        input_grad,
        summed[0],
        summed[1],
        summed[2],
        summed[3],
        summed[4],
        summed[5],
        gains_grad,
        biases_grad,
    )


def solution(mesh):
    in_specs = (
        P(("dp", "tensor"), None),
        P("dp"),
        P("dp", None, "tensor"),
        P(None, "tensor", "dp"),
        P("tensor", "dp"),
        P("dp", "tensor"),
        P("tensor", "dp"),
        P("tensor", "dp"),
        P(None, ("dp", "tensor")),
        P(None, ("dp", "tensor")),
        P(("dp", "tensor"), None),
    )
    out_specs = (
        P(("dp", "tensor"), None),
        P(("dp", "tensor"), None),
        P("dp", None, "tensor"),
        P(None, "tensor", "dp"),
        P("tensor", "dp"),
        P("dp", "tensor"),
        P("tensor", "dp"),
        P("tensor", "dp"),
        P(None, ("dp", "tensor")),
        P(None, ("dp", "tensor")),
    )
    return jax.shard_map(shards, mesh=mesh, in_specs=in_specs, out_specs=out_specs, check_vma=False)
```

profile of v0, /device:TPU:0, one launch (start us, length us, event | category | flops | bytes accessed | tf_op | source)
XLA Modules:
  0.0 1526.1 jit_solution(3073304048536600505)
XLA Ops:
  8.7 71.2 %all-gather = bf16[32,64,2]{1,2,0:T(2,128)(2,1)S(1)} all-gather(bf16[1,64,2]{1,2,0:T(2,128)(2,1)} %bitcast.182), channel_id=1, replica_groups=mesh['dp'=8,'tensor'=4] {'dp','tensor'}, dimensions={0}, use_global_device_ids=true | all-gather | bytes 8448 | tf_op jit(solution)/shard_map/all_gather | solution.py:152
  80.0 66.0 %all-gather.1 = bf16[32,64,4]{1,2,0:T(4,128)(2,1)S(1)} all-gather(bf16[1,64,4]{1,2,0:T(4,128)(2,1)} %bitcast.181), channel_id=1, replica_groups=mesh['dp'=8,'tensor'=4] {'dp','tensor'}, dimensions={0}, use_global_device_ids=true | all-gather | bytes 16896 | tf_op jit(solution)/shard_map/all_gather | solution.py:153
  155.9 8.2 all_gather.45
  164.7 9.5 all_gather.41
  177.6 6.2 convolution_convert_fusion.1
  183.8 47.5 %all-gather.10.cloned.1.call-done = bf16[1024,2048]{1,0:T(8,128)(2,1)} async-done(((bf16[256,2048]{1,0:T(8,128)(2,1)}), bf16[1024,2048]{1,0:T(8,128)(2,1)}) %all-gather.10.cloned.1.call-update) | async-done | bytes 4194320 | tf_op jit(solution)/shard_map/all_gather | solution.py:160
  231.3 47.4 %all-gather.12.cloned.1.call-done = bf16[2048,3,512]{0,2,1:T(8,128)(2,1)} async-done(((bf16[256,3,512]{0,2,1:T(8,128)(2,1)}), bf16[2048,3,512]{0,2,1:T(8,128)(2,1)}) %all-gather.12.cloned.1.call-update) | async-done | bytes 6291472 | tf_op jit(solution)/shard_map/all_gather | solution.py:143
  278.7 10.1 broadcast_add_fusion
  324.7 20.5 %while.27 = (s32[]{:T(128)}, bf16[2,512,2,256]{3,1,2,0:T(8,128)(2,1)}, f32[2,2,512]{2,1,0:T(2,128)S(1)}, s32[2]{0:T(128)S(1)}, s32[1024]{0:T(1024)S(1)}, /*index...) while((s32[]{:T(128)}, ...), condition=%wide.region_5.6_spmd, body=%wide.region_2.5_spmd.sunk | while | flops 1087897088 | bytes 26786032 | solution.py:78
  345.2 30.7 %while.28 = (s32[]{:T(128)}, f32[1024,2,256]{0,2,1:T(8,128)S(1)}, f32[1024,2,256]{0,2,1:T(8,128)}, f32[2,512,2,256]{3,1,0,2:T(8,128)}, s32[2]{0:T(128)S(1)}, /*i...) while((s32[]{:T(128)}, f32[1024,2,256]{0,2,1:T(8,128)S(1)}, ...), condition=%wide.region_12.13_spmd.clone, body=%wide.region_10.12_spmd.clone.sunk | while | flops 2704539136 | bytes 94415280 | solution.py:119
  394.5 11.4 bitcast_convert_fusion
  406.0 10.0 all-gather.18.cloned.1.call-done
  416.0 14.8 fusion.78
  430.8 42.9 %all-gather.20.cloned.1.call-done = bf16[2048,2048]{1,0:T(8,128)(2,1)} async-done(((bf16[2048,256]{1,0:T(8,128)(2,1)}), bf16[2048,2048]{1,0:T(8,128)(2,1)}) %all-gather.20.cloned.1.call-update) | async-done | bytes 8388624 | tf_op jit(solution)/shard_map/all_gather | solution.py:148
  473.8 33.0 %convert_reduce_fusion = (f32[2048]{0:T(1024)S(1)}, bf16[1024,2048]{1,0:T(8,128)(2,1)S(1)}, f32[1024,2048]{1,0:T(8,128)}) fusion(f32[1024,2048]{1,0:T(8,128)} %fusion.78, f32[2048]{0:T(1024)S(1)} %bitcast.166, bf16[1024,2048]{1,0:T(8,128)(2,1)} %all-gather.22.cloned.1.call-done, bf16[2048,2048]{1,0:T(8,128)(2,1)} %all-gather.20.cloned.1.call-done), kind=kOutput, calls=%fused_computation.50 | convolution fusion | flops 8747218944 | bytes 33570816 | tf_op jit(solution)/shard_map/nd,fd->nf/dot_general | solution.py:201
  508.7 10.9 convolution_convert_fusion
  522.2 10.0 multiply_convert_fusion.1
  532.2 12.7 fusion.79
  545.0 5.6 convolution_add_fusion
  556.6 75.9 %reduce-scatter.22.cloned.1.call-done = bf16[256,2048]{1,0:T(8,128)(2,1)} async-done(((bf16[1024,2048]{1,0:T(8,128)(2,1)}), bf16[256,2048]{1,0:T(8,128)(2,1)}) %reduce-scatter.22.cloned.1.call-update) | async-done | bytes 1048592 | tf_op jit(solution)/shard_map/reduce_scatter | solution.py:242
  640.1 139.7 %reduce-scatter.20.cloned.1.call-done = f32[256,2048]{1,0:T(8,128)} async-done(((f32[1024,2048]{1,0:T(8,128)}), f32[256,2048]{1,0:T(8,128)}) %reduce-scatter.20.cloned.1.call-update) | async-done | bytes 2097168 | tf_op jit(solution)/shard_map/reduce_scatter | solution.py:184
  786.6 6.5 fusion.80
  795.0 11.6 fusion.41
  806.7 15.3 %fusion.82 = f32[2048,2048]{1,0:T(8,128)} fusion(bf16[1024,2048]{1,0:T(8,128)(2,1)} %multiply_convert_fusion.1, bf16[1024,2048]{1,0:T(8,128)(2,1)} %all-gather.22.cloned.1.call-done), kind=kOutput, calls=%fused_computation.157 | convolution fusion | flops 8589934592 | bytes 25165824 | tf_op jit(solution)/shard_map/nf,nd->fd/dot_general | solution.py:202
  822.4 15.3 %fusion.81 = f32[2048,2048]{1,0:T(8,128)} fusion(bf16[1024,2048]{1,0:T(8,128)(2,1)} %all-gather.16.cloned.1.call-done, bf16[1024,2048]{1,0:T(8,128)(2,1)} %copy-done.45), kind=kOutput, calls=%fused_computation.156 | convolution fusion | flops 8589934592 | bytes 25165824 | tf_op jit(solution)/shard_map/nd,nf->df/dot_general | solution.py:205
  839.3 16.8 %reduce-scatter.36.cloned.1.call-done = f32[256,1]{1,0:T(8,128)} async-done(((f32[2048,1]{1,0:T(8,128)}), f32[256,1]{1,0:T(8,128)}) %reduce-scatter.36.cloned.1.call-update) | async-done | bytes 1040
  857.6 138.1 %reduce-scatter.38.cloned.1.call-done = f32[64,2]{1,0:T(8,128)} async-done(((f32[2048,2]{1,0:T(8,128)}), f32[64,2]{1,0:T(8,128)}) %reduce-scatter.38.cloned.1.call-update) | async-done | bytes 528
  997.1 134.3 %reduce-scatter.40.cloned.1.call-done = f32[64,4]{1,0:T(8,128)} async-done(((f32[2048,4]{1,0:T(8,128)}), f32[64,4]{1,0:T(8,128)}) %reduce-scatter.40.cloned.1.call-update) | async-done | bytes 1040
  1132.9 49.8 %reduce-scatter.28.cloned.1.call-done = f32[512,256]{1,0:T(8,128)} async-done(((f32[512,2048]{1,0:T(8,128)}), f32[512,256]{1,0:T(8,128)}) %reduce-scatter.28.cloned.1.call-update) | async-done | bytes 524304 | tf_op jit(solution)/shard_map/reduce_scatter | solution.py:258
  1182.7 96.0 %reduce-scatter.26.cloned.1.call-done = f32[256,3,512]{2,0,1:T(8,128)} async-done(((f32[2048,3,512]{2,0,1:T(8,128)}), f32[256,3,512]{2,0,1:T(8,128)}) %reduce-scatter.26.cloned.1.call-update) | async-done | bytes 1572880 | tf_op jit(solution)/shard_map/reduce_scatter | solution.py:256
  1278.8 120.0 %reduce-scatter.32.cloned.1.call-done = f32[2048,256]{1,0:T(8,128)} async-done(((f32[2048,2048]{1,0:T(8,128)}), f32[2048,256]{1,0:T(8,128)}) %reduce-scatter.32.cloned.1.call-update) | async-done | bytes 2097168 | tf_op jit(solution)/shard_map/reduce_scatter | solution.py:261
  1398.8 120.2 %reduce-scatter.30.cloned.1.call-done = f32[256,2048]{1,0:T(8,128)} async-done(((f32[2048,2048]{1,0:T(8,128)}), f32[256,2048]{1,0:T(8,128)}) %reduce-scatter.30.cloned.1.call-update) | async-done | bytes 2097168 | tf_op jit(solution)/shard_map/reduce_scatter | solution.py:259
  (267 shorter events, 145.4 us)
Async XLA Ops:
  7.2 143.3 %copy-start.1 = (bf16[256,2048]{1,0:T(8,128)(2,1)S(1)}, bf16[256,2048]{1,0:T(8,128)(2,1)}, u32[]{:S(2)}) copy-start(bf16[256,2048]{1,0:T(8,128)(2,1)} %param.15) | copy-start | bytes 3145732
  7.2 145.4 %copy-start.28 = (bf16[256,3,512]{2,0,1:T(8,128)(2,1)S(1)}, bf16[256,3,512]{2,0,1:T(8,128)(2,1)}, u32[]{:S(2)}) copy-start(bf16[256,3,512]{2,0,1:T(8,128)(2,1)} %param.17) | copy-start | bytes 2359300
  7.2 170.4 %all-gather.14.cloned.1.call-start = ((), (), s32[]{:S(2)}) async-start(), calls=%async_computation.13 | async-start | bytes 2359296 | tf_op jit(solution)/shard_map/all_gather | solution.py:145
  7.9 169.6 %all-gather.22.cloned.1.call-start = ((), (), s32[]{:S(2)}) async-start(), calls=%async_computation.18 | async-start | bytes 5242880 | tf_op jit(solution)/shard_map/all_gather | solution.py:191
  8.7 222.6 %all-gather.10.cloned.1.call-start = ((), (), s32[]{:S(2)}) async-start(), calls=%async_computation.11 | async-start | bytes 5242880 | tf_op jit(solution)/shard_map/all_gather | solution.py:160
  152.5 21.9 %copy-start.24 = (s32[1024]{0:T(1024)S(1)}, s32[1024]{0:T(1024)}, u32[]{:S(2)}) copy-start(s32[1024]{0:T(1024)} %param.16) | copy-start | bytes 12292
  152.5 126.2 %all-gather.12.cloned.1.call-start = ((), (), s32[]{:S(2)}) async-start(), calls=%async_computation.12 | async-start | bytes 7077888 | tf_op jit(solution)/shard_map/all_gather | solution.py:143
  153.8 252.2 %all-gather.16.cloned.1.call-start = ((), (), s32[]{:S(2)}) async-start(), calls=%async_computation.14 | async-start | bytes 5242880 | tf_op jit(solution)/shard_map/all_gather | solution.py:161
  154.4 261.6 %all-gather.18.cloned.1.call-start = ((), (), s32[]{:S(2)}) async-start(), calls=%async_computation.15 | async-start | bytes 9437184 | tf_op jit(solution)/shard_map/all_gather | solution.py:146
  155.0 318.8 %all-gather.20.cloned.1.call-start = ((), (), s32[]{:S(2)}) async-start(), calls=%async_computation.16 | async-start | bytes 9437184 | tf_op jit(solution)/shard_map/all_gather | solution.py:148
  155.7 400.8 %reduce-scatter.24.cloned.1.call-start = ((), (), s32[]{:S(2)}) async-start(), calls=%async_computation.20 | async-start | bytes 5242880 | tf_op jit(solution)/shard_map/reduce_scatter | solution.py:239
  405.9 67.9 %copy-start.35 = (f32[1,2048]{1,0:T(1,128)S(1)}, f32[1,2048]{1,0:T(1,128)}, u32[]{:S(2)}) copy-start(f32[1,2048]{1,0:T(1,128)} %add.225) | copy-start | bytes 24580
  405.9 226.6 %reduce-scatter.22.cloned.1.call-start = ((), (), s32[]{:S(2)}) async-start(), calls=%async_computation.19 | async-start | bytes 5242880 | tf_op jit(solution)/shard_map/reduce_scatter | solution.py:242
  473.8 35.0 %copy-start.44 = (bf16[2048,2048]{1,0:T(8,128)(2,1)S(1)}, bf16[2048,2048]{1,0:T(8,128)(2,1)}, u32[]{:S(2)}) copy-start(bf16[2048,2048]{1,0:T(8,128)(2,1)} %all-gather.18.cloned.1.call-done) | copy-start | bytes 25165828
  519.7 260.2 %reduce-scatter.20.cloned.1.call-start = ((), (), s32[]{:S(2)}) async-start(), calls=%async_computation.17 | async-start | bytes 10485760 | tf_op jit(solution)/shard_map/reduce_scatter | solution.py:184
  550.6 81.9 %copy-start.2 = (bf16[256,2048]{1,0:T(8,128)(2,1)S(1)}, bf16[256,2048]{1,0:T(8,128)(2,1)}, u32[]{:S(2)}) copy-start(bf16[256,2048]{1,0:T(8,128)(2,1)} %param.15) | copy-start | bytes 3145732
  550.6 81.9 %copy-start.30 = (f32[1,2048]{1,0:T(1,128)S(1)}, f32[1,2048]{1,0:T(1,128)}, u32[]{:S(2)}) copy-start(f32[1,2048]{1,0:T(1,128)} %copy-done.29) | copy-start | bytes 24580
  550.6 81.9 %copy-start.32 = (f32[1,2048]{1,0:T(1,128)S(1)}, f32[1,2048]{1,0:T(1,128)}, u32[]{:S(2)}) copy-start(f32[1,2048]{1,0:T(1,128)} %copy-done.31) | copy-start | bytes 24580
  550.6 81.9 %copy-start.34 = (f32[256]{0:T(256)S(1)}, f32[256]{0:T(256)}, u32[]{:S(2)}) copy-start(f32[256]{0:T(256)} %copy-done.33) | copy-start | bytes 3076
  550.7 84.6 %copy-start.41 = (f32[256]{0:T(256)S(1)}, f32[256]{0:T(256)}, u32[]{:S(2)}) copy-start(f32[256]{0:T(256)} %copy-done.40) | copy-start | bytes 3076
  550.7 84.6 %copy-start.39 = (f32[256]{0:T(256)S(1)}, f32[256]{0:T(256)}, u32[]{:S(2)}) copy-start(f32[256]{0:T(256)} %copy-done.38) | copy-start | bytes 3076
  550.7 287.1 %reduce-scatter.34.cloned.1.call-start = ((), (), s32[]{:S(2)}) async-start(), calls=%async_computation.25 | async-start | bytes 147456
  555.0 301.0 %reduce-scatter.36.cloned.1.call-start = ((), (), s32[]{:S(2)}) async-start(), calls=%async_computation.26 | async-start | bytes 1179648
  556.5 223.4 %copy-start.36 = (f32[1,2048]{1,0:T(1,128)S(1)}, f32[1,2048]{1,0:T(1,128)}, u32[]{:S(2)}) copy-start(f32[1,2048]{1,0:T(1,128)} %get-tuple-element.328) | copy-start | bytes 24580
  556.5 223.4 %copy-start.37 = (f32[1,2048]{1,0:T(1,128)S(1)}, f32[1,2048]{1,0:T(1,128)}, u32[]{:S(2)}) copy-start(f32[1,2048]{1,0:T(1,128)} %get-tuple-element.329) | copy-start | bytes 24580
  556.5 439.3 %reduce-scatter.38.cloned.1.call-start = ((), (), s32[]{:S(2)}) async-start(), calls=%async_computation.27 | async-start | bytes 1081344
  556.6 223.3 %copy-start.4 = (bf16[256,2048]{1,0:T(8,128)(2,1)S(1)}, bf16[256,2048]{1,0:T(8,128)(2,1)}, u32[]{:S(2)}) copy-start(bf16[256,2048]{1,0:T(8,128)(2,1)} %reduce-scatter.24.cloned.1.call-done) | copy-start | bytes 3145732
  640.1 491.4 %reduce-scatter.40.cloned.1.call-start = ((), (), s32[]{:S(2)}) async-start(), calls=%async_computation.28 | async-start | bytes 1081344
  786.3 396.4 %reduce-scatter.28.cloned.1.call-start = ((), (), s32[]{:S(2)}) async-start(), calls=%async_computation.22 | async-start | bytes 4718592 | tf_op jit(solution)/shard_map/reduce_scatter | solution.py:258
  793.2 485.6 %reduce-scatter.26.cloned.1.call-start = ((), (), s32[]{:S(2)}) async-start(), calls=%async_computation.21 | async-start | bytes 14155776 | tf_op jit(solution)/shard_map/reduce_scatter | solution.py:256
  806.7 592.1 %reduce-scatter.32.cloned.1.call-start = ((), (), s32[]{:S(2)}) async-start(), calls=%async_computation.24 | async-start | bytes 18874368 | tf_op jit(solution)/shard_map/reduce_scatter | solution.py:261
  822.1 696.9 %reduce-scatter.30.cloned.1.call-start = ((), (), s32[]{:S(2)}) async-start(), calls=%async_computation.23 | async-start | bytes 18874368 | tf_op jit(solution)/shard_map/reduce_scatter | solution.py:259
  (41 other events, 152.7 us)
Sparse Core Ops, SparseCore 0:
  9.9 30.8 all-gather.13
  42.3 81.0 all-gather.21
  152.7 78.5 all-gather.9
  233.6 45.0 all-gather.11
  280.7 80.7 all-gather.15
  363.2 52.7 all-gather.17
  417.9 55.8 all-gather.19
  476.0 76.7 reduce-scatter.23
  555.2 77.2 reduce-scatter.21
  634.7 145.1 reduce-scatter.19
  782.9 34.1 reduce-scatter.33
  820.1 35.9 reduce-scatter.35
  858.3 137.3 reduce-scatter.37
  997.9 133.5 reduce-scatter.39
  1135.3 47.4 reduce-scatter.27
  1186.7 92.0 reduce-scatter.25
  1282.8 115.9 reduce-scatter.31
  1402.8 116.1 reduce-scatter.29
where the time goes:
time: 1530 us
  waiting for transfers between devices  1040 us (68%)
  matrix products  177 us (12%)
  blocking collectives  155 us (10%)
  local copies, waits for them, and re-layouts  69 us (5%)
  other arithmetic  58 us (4%)
    unnamed x22, waiting for transfers between devices  293 us
    reduce_scatter x1, waiting for transfers between devices, shards(): lax.psum_scatter(attn_part + jnp.dot(activated, back_weight, preferred_el...  140 us
    reduce_scatter x1, waiting for transfers between devices, shards(): lax.psum_scatter(up_term, 'dp', scatter_dimension=0, tiled=True)  120 us
    reduce_scatter x1, waiting for transfers between devices, shards(): lax.psum_scatter(down_term, 'dp', scatter_dimension=1, tiled=True)  120 us
    reduce_scatter x1, waiting for transfers between devices, shards(): lax.psum_scatter(joined_term, 'dp', scatter_dimension=0, tiled=True)  96 us
    reduce_scatter x1, waiting for transfers between devices, shards(): lax.psum_scatter(grad_second.astype(jnp.bfloat16), 'tensor', scatter_dime...  75.9 us
    all_gather x1, blocking collectives, shards(): lax.all_gather(norm_gains, ('dp', 'tensor'), axis=1, tiled=True)  71.2 us
    all_gather x1, blocking collectives, shards(): lax.all_gather(biases, ('dp', 'tensor'), axis=1, tiled=True)  66 us
  transfers between devices with their start and end apart: 18, of which 13 were waited for; matrix products, arithmetic and copies ran while one was open for 19% of the time, Pallas kernels for 0%

commit v1 on v0

--- a/solution.py
+++ b/solution.py
@@ -6,6 +6,36 @@
 ROT = 64
 EPSILON = 1e-05
 ROTARY_BASE = 10000.0
+
+
+def obtain_page(local, dim_i):
+    local = jnp.moveaxis(local, 0, dim_i)
+    field_out = local.shape
+    seen_now = local.reshape(
+        *field_out[:dim_i], field_out[dim_i] * field_out[dim_i + 1], *field_out[dim_i + 2 :]
+    )
+    return seen_now
+
+
+def carry_views(x_local, lane_axis):
+    n_chips = jax.lax.axis_size(lane_axis)
+    y_new = x_local[None]
+    for h in range(n_chips.bit_length() - 1):
+        wide_out = 1 << h
+        response = jax.lax.ppermute(
+            y_new, axis_name=lane_axis, perm=[(u, u ^ wide_out) for u in range(n_chips)]
+        )
+        item_now = jnp.stack([y_new, response])
+        main = jax.lax.axis_index(lane_axis)
+        tall = main >> h & 1
+        y_new = jnp.where(tall == 0, item_now, item_now[::-1]).reshape(-1, *x_local.shape)
+    return y_new
+
+
+def follow_lots_all_now(state, m, at_axis):
+    d_next = carry_views(state, m)
+    passed = obtain_page(d_next, at_axis)
+    return passed
 
 
 def layer_norm(values, gain_row, shift_row):
@@ -145,7 +175,7 @@
         lax.all_gather(out_weight, "dp", axis=1, tiled=True),
         lax.all_gather(up_weight, "dp", axis=0, tiled=True),
         lax.all_gather(up_bias, "dp", axis=1, tiled=True),
-        lax.all_gather(down_weight, "dp", axis=1, tiled=True),
+        follow_lots_all_now(down_weight, "dp", 1),
     )
     joined_weight, joined_bias, mix_weight, hidden_weight, hidden_bias, back_weight = gathered
     gain_rows, shift_rows = (

time: 1530 us -> 1560 us (1.020)
  waiting for transfers between devices: 1040 us -> 985 us
  blocking collectives: 155 us -> 197 us
  other arithmetic: 58 us -> 82.4 us
  matrix products: 177 us -> 193 us
    all_gather x1, waiting for transfers between devices: 47.5 us -> 0.01 us  [shards(): lax.all_gather(first_local.astype(jnp.bfloat16), 'tensor', axis=0, tiled=...]
    all_gather x1, blocking collectives: 9.5 us -> 51.3 us  [shards(): lax.all_gather(proj_bias, 'dp', axis=2, tiled=True)]
    reduce_scatter x1, waiting for transfers between devices: 75.9 us -> 45.1 us  [shards(): lax.psum_scatter(grad_second.astype(jnp.bfloat16), 'tensor', scatter_dime...]
    select_n x0 -> x2, other arithmetic: none -> 17.2 us  [carry_views(): jnp.where(tall == 0, item_now, item_now[::-1]).reshape(-1, *x_local.shape)]
    unnamed x94 -> x102, local copies, waits for them, and re-layouts: 34.8 us -> 29.3 us
  transfers between devices with their start and end apart: 18 -> 21, of which waited for: 13 -> 13; matrix products, arithmetic and copies ran while one was open for 19% -> 21% of each run, Pallas kernels for 0% -> 0%
where the time goes in v1:
time: 1560 us; the launch traced here: 1550 us
  waiting for transfers between devices  985 us (63%)
  blocking collectives  197 us (13%)
  matrix products  193 us (12%)
  other arithmetic  82.4 us (5%)
  local copies, waits for them, and re-layouts  68.2 us (4%)
    unnamed x22, waiting for transfers between devices  292 us
    reduce_scatter x1, waiting for transfers between devices, shards(): lax.psum_scatter(attn_part + jnp.dot(activated, back_weight, preferred_el...  140 us
    reduce_scatter x1, waiting for transfers between devices, shards(): lax.psum_scatter(up_term, 'dp', scatter_dimension=0, tiled=True)  120 us
    reduce_scatter x1, waiting for transfers between devices, shards(): lax.psum_scatter(down_term, 'dp', scatter_dimension=1, tiled=True)  120 us
    reduce_scatter x1, waiting for transfers between devices, shards(): lax.psum_scatter(joined_term, 'dp', scatter_dimension=0, tiled=True)  96 us
    all_gather x1, blocking collectives, shards(): lax.all_gather(norm_gains, ('dp', 'tensor'), axis=1, tiled=True)  71.2 us
    all_gather x1, blocking collectives, shards(): lax.all_gather(biases, ('dp', 'tensor'), axis=1, tiled=True)  66 us
    all_gather x1, waiting for transfers between devices, shards(): lax.all_gather(proj_weight, 'dp', axis=0, tiled=True)  61 us
  transfers between devices with their start and end apart: 21, of which 13 were waited for; matrix products, arithmetic and copies ran while one was open for 21% of the time, Pallas kernels for 0%

profile of v1, /device:TPU:0, one launch (start us, length us, event | category | flops | bytes accessed | tf_op | source)
XLA Modules:
  0.0 1551.0 jit_solution(11538713949443641602)
XLA Ops:
  8.7 71.2 %all-gather = bf16[32,64,2]{1,2,0:T(2,128)(2,1)S(1)} all-gather(bf16[1,64,2]{1,2,0:T(2,128)(2,1)} %bitcast.204), channel_id=1, replica_groups=mesh['dp'=8,'tensor'=4] {'dp','tensor'}, dimensions={0}, use_global_device_ids=true | all-gather | bytes 8448 | tf_op jit(solution)/shard_map/all_gather | solution.py:182
  80.0 66.0 %all-gather.1 = bf16[32,64,4]{1,2,0:T(4,128)(2,1)S(1)} all-gather(bf16[1,64,4]{1,2,0:T(4,128)(2,1)} %bitcast.203), channel_id=1, replica_groups=mesh['dp'=8,'tensor'=4] {'dp','tensor'}, dimensions={0}, use_global_device_ids=true | all-gather | bytes 16896 | tf_op jit(solution)/shard_map/all_gather | solution.py:183
  160.1 51.3 %all_gather.40 = bf16[3,2,256]{0,1,2:T(2,128)(2,1)S(1)} all-gather(bf16[3,2,32]{0,1,2:T(2,128)(2,1)S(1)} %copy.125), channel_id=1, replica_groups=mesh['dp'=8,'tensor'=4] {'dp'}, dimensions={2}, use_global_device_ids=true | all-gather | bytes 3456 | tf_op jit(solution)/shard_map/all_gather | solution.py:174
  211.5 8.9 all_gather.44
  242.6 61.0 %all-gather.12.cloned.1.call-done = bf16[2048,3,512]{0,2,1:T(8,128)(2,1)} async-done(((bf16[256,3,512]{0,2,1:T(8,128)(2,1)}), bf16[2048,3,512]{0,2,1:T(8,128)(2,1)}) %all-gather.12.cloned.1.call-update) | async-done | bytes 6291472 | tf_op jit(solution)/shard_map/all_gather | solution.py:173
  303.6 10.1 broadcast_add_fusion
  333.4 19.8 %while.27 = (s32[]{:T(128)}, bf16[2,512,2,256]{3,1,2,0:T(8,128)(2,1)}, f32[2,2,512]{2,1,0:T(2,128)S(1)}, s32[2]{0:T(128)S(1)}, s32[1024]{0:T(1024)S(1)}, /*index...) while((s32[]{:T(128)}, ...), condition=%wide.region_5.6_spmd, body=%wide.region_2.5_spmd.sunk | while | flops 1087897088 | bytes 18397868 | solution.py:108
  353.3 40.5 %while.28 = (s32[]{:T(128)}, f32[1024,2,256]{0,2,1:T(8,128)}, f32[1024,2,256]{0,2,1:T(8,128)}, f32[2,512,2,256]{3,1,0,2:T(8,128)}, s32[2]{0:T(128)S(1)}, /*index...) while((s32[]{:T(128)}, f32[1024,2,256]{0,2,1:T(8,128)}, ...), condition=%wide.region_12.13_spmd.clone, body=%wide.region_10.12_spmd.clone.sunk | while | flops 2704539136 | bytes 123775488 | solution.py:149
  413.0 12.7 bitcast_convert_fusion
  425.8 15.1 all-gather.18.cloned.1.call-done
  440.9 14.6 fusion.81
  455.5 43.2 %all-gather.22.cloned.1.call-done = bf16[2048,2048]{1,0:T(8,128)(2,1)} async-done(((bf16[2048,256]{1,0:T(8,128)(2,1)}), bf16[2048,2048]{1,0:T(8,128)(2,1)}) %all-gather.22.cloned.1.call-update) | async-done | bytes 8388624 | tf_op jit(solution)/shard_map/all_gather | solution.py:228
  498.7 33.1 %convert_reduce_fusion = (f32[2048]{0:T(1024)S(1)}, bf16[1024,2048]{1,0:T(8,128)(2,1)S(1)}, f32[1024,2048]{1,0:T(8,128)}) fusion(f32[1024,2048]{1,0:T(8,128)} %fusion.81, f32[2048]{0:T(1024)S(1)} %bitcast.188, bf16[1024,2048]{1,0:T(8,128)(2,1)} %all-gather.20.cloned.1.call-done, bf16[2048,2048]{1,0:T(8,128)(2,1)} %all-gather.22.cloned.1.call-done), kind=kOutput, calls=%fused_computation.52 | convolution fusion | flops 8747218944 | bytes 33570816 | tf_op jit(solution)/shard_map/nd,fd->nf/dot_general | solution.py:231
  533.7 10.5 convolution_convert_fusion
  544.3 6.7 copy.136
  551.0 7.6 pad_maximum_fusion
  558.6 14.3 reverse_select_fusion
  581.2 8.4 multiply_convert_fusion.1
  591.6 14.7 convolution_add_fusion
  612.3 45.1 %reduce-scatter.22.cloned.1.call-done = bf16[256,2048]{1,0:T(8,128)(2,1)} async-done(((bf16[1024,2048]{1,0:T(8,128)(2,1)}), bf16[256,2048]{1,0:T(8,128)(2,1)}) %reduce-scatter.22.cloned.1.call-update) | async-done | bytes 1048592 | tf_op jit(solution)/shard_map/reduce_scatter | solution.py:272
  665.2 139.6 %reduce-scatter.20.cloned.1.call-done = f32[256,2048]{1,0:T(8,128)} async-done(((f32[1024,2048]{1,0:T(8,128)}), f32[256,2048]{1,0:T(8,128)}) %reduce-scatter.20.cloned.1.call-update) | async-done | bytes 2097168 | tf_op jit(solution)/shard_map/reduce_scatter | solution.py:214
  811.3 6.9 fusion.82
  820.1 11.9 fusion.41
  832.0 15.2 fusion.84
  847.3 15.2 fusion.83
  864.1 16.9 %reduce-scatter.36.cloned.1.call-done = f32[256,1]{1,0:T(8,128)} async-done(((f32[2048,1]{1,0:T(8,128)}), f32[256,1]{1,0:T(8,128)}) %reduce-scatter.36.cloned.1.call-update) | async-done | bytes 1040
  882.6 138.1 %reduce-scatter.38.cloned.1.call-done = f32[64,2]{1,0:T(8,128)} async-done(((f32[2048,2]{1,0:T(8,128)}), f32[64,2]{1,0:T(8,128)}) %reduce-scatter.38.cloned.1.call-update) | async-done | bytes 528
  1022.1 134.5 %reduce-scatter.40.cloned.1.call-done = f32[64,4]{1,0:T(8,128)} async-done(((f32[2048,4]{1,0:T(8,128)}), f32[64,4]{1,0:T(8,128)}) %reduce-scatter.40.cloned.1.call-update) | async-done | bytes 1040
  1158.0 49.7 %reduce-scatter.28.cloned.1.call-done = f32[512,256]{1,0:T(8,128)} async-done(((f32[512,2048]{1,0:T(8,128)}), f32[512,256]{1,0:T(8,128)}) %reduce-scatter.28.cloned.1.call-update) | async-done | bytes 524304 | tf_op jit(solution)/shard_map/reduce_scatter | solution.py:288
  1207.7 96.0 %reduce-scatter.26.cloned.1.call-done = f32[256,3,512]{2,0,1:T(8,128)} async-done(((f32[2048,3,512]{2,0,1:T(8,128)}), f32[256,3,512]{2,0,1:T(8,128)}) %reduce-scatter.26.cloned.1.call-update) | async-done | bytes 1572880 | tf_op jit(solution)/shard_map/reduce_scatter | solution.py:286
  1303.7 120.0 %reduce-scatter.32.cloned.1.call-done = f32[2048,256]{1,0:T(8,128)} async-done(((f32[2048,2048]{1,0:T(8,128)}), f32[2048,256]{1,0:T(8,128)}) %reduce-scatter.32.cloned.1.call-update) | async-done | bytes 2097168 | tf_op jit(solution)/shard_map/reduce_scatter | solution.py:291
  1423.7 120.2 %reduce-scatter.30.cloned.1.call-done = f32[256,2048]{1,0:T(8,128)} async-done(((f32[2048,2048]{1,0:T(8,128)}), f32[256,2048]{1,0:T(8,128)}) %reduce-scatter.30.cloned.1.call-update) | async-done | bytes 2097168 | tf_op jit(solution)/shard_map/reduce_scatter | solution.py:289
  (293 shorter events, 168.6 us)
Async XLA Ops:
  7.2 143.3 %copy-start.6 = (bf16[256,2048]{1,0:T(8,128)(2,1)S(1)}, bf16[256,2048]{1,0:T(8,128)(2,1)}, u32[]{:S(2)}) copy-start(bf16[256,2048]{1,0:T(8,128)(2,1)} %param.15) | copy-start | bytes 3145732
  7.2 145.4 %copy-start.32 = (bf16[256,3,512]{2,0,1:T(8,128)(2,1)S(1)}, bf16[256,3,512]{2,0,1:T(8,128)(2,1)}, u32[]{:S(2)}) copy-start(bf16[256,3,512]{2,0,1:T(8,128)(2,1)} %param.17) | copy-start | bytes 2359300
  7.2 228.9 %all-gather.14.cloned.1.call-start = ((), (), s32[]{:S(2)}) async-start(), calls=%async_computation.13 | async-start | bytes 2359296 | tf_op jit(solution)/shard_map/all_gather | solution.py:175
  7.9 228.2 %all-gather.20.cloned.1.call-start = ((), (), s32[]{:S(2)}) async-start(), calls=%async_computation.17 | async-start | bytes 5242880 | tf_op jit(solution)/shard_map/all_gather | solution.py:221
  8.7 233.9 %all-gather.10.cloned.1.call-start = ((), (), s32[]{:S(2)}) async-start(), calls=%async_computation.11 | async-start | bytes 5242880 | tf_op jit(solution)/shard_map/all_gather | solution.py:190
  152.6 151.1 %all-gather.12.cloned.1.call-start = ((), (), s32[]{:S(2)}) async-start(), calls=%async_computation.12 | async-start | bytes 7077888 | tf_op jit(solution)/shard_map/all_gather | solution.py:173
  153.8 272.1 %all-gather.16.cloned.1.call-start = ((), (), s32[]{:S(2)}) async-start(), calls=%async_computation.14 | async-start | bytes 5242880 | tf_op jit(solution)/shard_map/all_gather | solution.py:191
  154.4 286.5 %all-gather.18.cloned.1.call-start = ((), (), s32[]{:S(2)}) async-start(), calls=%async_computation.15 | async-start | bytes 9437184 | tf_op jit(solution)/shard_map/all_gather | solution.py:176
  155.0 343.7 %all-gather.22.cloned.1.call-start = ((), (), s32[]{:S(2)}) async-start(), calls=%async_computation.18 | async-start | bytes 9437184 | tf_op jit(solution)/shard_map/all_gather | solution.py:228
  155.0 2.7 collective-permute-start
  158.0 53.5 %copy-start.47 = (bf16[1,256]{1,0:T(2,128)(2,1)S(1)}, bf16[1,256]{1,0:T(2,128)(2,1)}, u32[]{:S(2)}) copy-start(bf16[1,256]{1,0:T(2,128)(2,1)} %param.21) | copy-start | bytes 1540
  158.0 63.0 %copy-start.31 = (s32[1024]{0:T(1024)S(1)}, s32[1024]{0:T(1024)}, u32[]{:S(2)}) copy-start(s32[1024]{0:T(1024)} %param.16) | copy-start | bytes 12292
  159.8 64.3 %collective-permute-start.1 = (bf16[2,2048,256]{2,1,0:T(8,128)(2,1)}, bf16[2,2048,256]{2,1,0:T(8,128)(2,1)}, u32[]{:S(2)}, u32[]{:S(2)}) collective-permute-start(bf16[2,2048,256]{2,1,0:T(8,128)(2,1)} %get-tuple-element.316), channel_id=1, source_target_pairs={{0,8},{4,12},{8,0},{12,4},{16,24},{20,28},{24,16},{28,20},{1,9},{5... | collective-permute-start | bytes 6291464 | tf_op jit(solution)/shard_map/ppermute | solution.py:25
  159.9 452.4 %reduce-scatter.24.cloned.1.call-start = ((), (), s32[]{:S(2)}) async-start(), calls=%async_computation.20 | async-start | bytes 5242880 | tf_op jit(solution)/shard_map/reduce_scatter | solution.py:269
  235.3 315.7 %collective-permute-start.2 = (bf16[4,2048,256]{1,2,0:T(8,128)(2,1)}, bf16[4,2048,256]{1,2,0:T(8,128)(2,1)}, u32[]{:S(2)}, u32[]{:S(2)}) collective-permute-start(bf16[4,2048,256]{1,2,0:T(8,128)(2,1)} %copy.135), channel_id=1, source_target_pairs={{0,16},{4,20},{8,24},{12,28},{16,0},{20,4},{24,8},{28,12},{1,17},{... | collective-permute-start | bytes 12582920 | tf_op jit(solution)/shard_map/ppermute | solution.py:25
  425.8 72.9 %copy-start.39 = (f32[1,2048]{1,0:T(1,128)S(1)}, f32[1,2048]{1,0:T(1,128)}, u32[]{:S(2)}) copy-start(f32[1,2048]{1,0:T(1,128)} %add.225) | copy-start | bytes 24580
  425.8 231.6 %reduce-scatter.22.cloned.1.call-start = ((), (), s32[]{:S(2)}) async-start(), calls=%async_computation.19 | async-start | bytes 5242880 | tf_op jit(solution)/shard_map/reduce_scatter | solution.py:272
  544.3 260.5 %reduce-scatter.20.cloned.1.call-start = ((), (), s32[]{:S(2)}) async-start(), calls=%async_computation.16 | async-start | bytes 10485760 | tf_op jit(solution)/shard_map/reduce_scatter | solution.py:214
  606.4 53.9 %copy-start.45 = (f32[256]{0:T(256)S(1)}, f32[256]{0:T(256)}, u32[]{:S(2)}) copy-start(f32[256]{0:T(256)} %copy-done.44) | copy-start | bytes 3076
  606.4 53.9 %copy-start.43 = (f32[256]{0:T(256)S(1)}, f32[256]{0:T(256)}, u32[]{:S(2)}) copy-start(f32[256]{0:T(256)} %copy-done.42) | copy-start | bytes 3076
  606.4 256.2 %reduce-scatter.34.cloned.1.call-start = ((), (), s32[]{:S(2)}) async-start(), calls=%async_computation.25 | async-start | bytes 147456
  610.8 270.3 %reduce-scatter.36.cloned.1.call-start = ((), (), s32[]{:S(2)}) async-start(), calls=%async_computation.26 | async-start | bytes 1179648
  612.2 192.6 %copy-start.40 = (f32[1,2048]{1,0:T(1,128)S(1)}, f32[1,2048]{1,0:T(1,128)}, u32[]{:S(2)}) copy-start(f32[1,2048]{1,0:T(1,128)} %get-tuple-element.330) | copy-start | bytes 24580
  612.2 192.6 %copy-start.41 = (f32[1,2048]{1,0:T(1,128)S(1)}, f32[1,2048]{1,0:T(1,128)}, u32[]{:S(2)}) copy-start(f32[1,2048]{1,0:T(1,128)} %get-tuple-element.331) | copy-start | bytes 24580
  612.2 408.5 %reduce-scatter.38.cloned.1.call-start = ((), (), s32[]{:S(2)}) async-start(), calls=%async_computation.27 | async-start | bytes 1081344
  612.3 192.5 %copy-start.8 = (bf16[256,2048]{1,0:T(8,128)(2,1)S(1)}, bf16[256,2048]{1,0:T(8,128)(2,1)}, u32[]{:S(2)}) copy-start(bf16[256,2048]{1,0:T(8,128)(2,1)} %reduce-scatter.24.cloned.1.call-done) | copy-start | bytes 3145732
  657.4 147.4 %copy-start.9 = (bf16[256,2048]{1,0:T(8,128)(2,1)S(1)}, bf16[256,2048]{1,0:T(8,128)(2,1)}, u32[]{:S(2)}) copy-start(bf16[256,2048]{1,0:T(8,128)(2,1)} %reduce-scatter.22.cloned.1.call-done) | copy-start | bytes 3145732
  665.1 491.5 %reduce-scatter.40.cloned.1.call-start = ((), (), s32[]{:S(2)}) async-start(), calls=%async_computation.28 | async-start | bytes 1081344
  811.3 396.4 %reduce-scatter.28.cloned.1.call-start = ((), (), s32[]{:S(2)}) async-start(), calls=%async_computation.22 | async-start | bytes 4718592 | tf_op jit(solution)/shard_map/reduce_scatter | solution.py:288
  818.2 485.5 %reduce-scatter.26.cloned.1.call-start = ((), (), s32[]{:S(2)}) async-start(), calls=%async_computation.21 | async-start | bytes 14155776 | tf_op jit(solution)/shard_map/reduce_scatter | solution.py:286
  832.0 591.7 %reduce-scatter.32.cloned.1.call-start = ((), (), s32[]{:S(2)}) async-start(), calls=%async_computation.24 | async-start | bytes 18874368 | tf_op jit(solution)/shard_map/reduce_scatter | solution.py:291
  847.3 696.7 %reduce-scatter.30.cloned.1.call-start = ((), (), s32[]{:S(2)}) async-start(), calls=%async_computation.23 | async-start | bytes 18874368 | tf_op jit(solution)/shard_map/reduce_scatter | solution.py:289
  (50 other events, 447.4 us)
Sparse Core Ops, SparseCore 0:
  9.9 30.8 all-gather.13
  42.3 81.0 all-gather.19
  152.7 78.5 all-gather.9
  233.0 70.5 all-gather.11
  305.6 80.7 all-gather.15
  388.1 52.7 all-gather.17
  442.8 55.8 all-gather.21
  501.0 76.7 reduce-scatter.23
  580.1 77.2 reduce-scatter.21
  659.6 145.1 reduce-scatter.19
  807.8 34.1 reduce-scatter.33
  845.0 35.9 reduce-scatter.35
  883.3 137.3 reduce-scatter.37
  1022.8 133.7 reduce-scatter.39
  1160.3 47.2 reduce-scatter.27
  1211.6 92.0 reduce-scatter.25
  1307.7 115.9 reduce-scatter.31
  1427.7 116.1 reduce-scatter.29
